TPU v7x, 32 devices: a whole 2x2x4 slice. The times are simulated.
32 devices in a mesh: dp: 8 (over z, x), seq: 4 (over y, core).
Axes of the slice: x: 2, y: 2, z: 4, core: 2. Of those that a mesh axis runs over, the one named last changes fastest.
Arguments:
- tokens: bfloat16 [16384, 1024], P(('dp', 'seq')), may hold values from -6 to 6
- time_embed: bfloat16 [32, 1024], P(('dp', 'seq')), may hold values from -6 to 6
- lengths: int32 [32], P('dp'), may hold values from 0 to 475, as said below
- cotangent: bfloat16 [16384, 1024], P(('dp', 'seq')), may hold values from -6 to 6
- w_query: bfloat16 [1024, 1024], P('seq'), may hold values from -0.1875 to 0.1875
- w_key: bfloat16 [1024, 1024], P('seq'), may hold values from -0.1875 to 0.1875
- w_value: bfloat16 [1024, 1024], P('seq'), may hold values from -0.1875 to 0.1875
- w_out: bfloat16 [1024, 1024], P('seq'), may hold values from -0.75 to 0.75
- w_time: bfloat16 [1024, 1024], P('seq'), may hold values from -0.1875 to 0.1875
- w_in: bfloat16 [4096, 1024], P('seq'), may hold values from -0.1875 to 0.1875
- w_down: bfloat16 [4096, 1024], P('seq'), may hold values from -0.09375 to 0.09375
- b_query: bfloat16 [1024], replicated, may hold values from -3 to 3
- b_value: bfloat16 [1024], replicated, may hold values from -3 to 3
- b_out: bfloat16 [1024], replicated, may hold values from -3 to 3
- b_time: bfloat16 [1024], replicated, may hold values from -3 to 3
- b_in: bfloat16 [4096], replicated, may hold values from -3 to 3
- b_down: bfloat16 [1024], replicated, may hold values from -2 to 2
- gain_one: bfloat16 [1024], replicated, may hold values from 0.25 to 1.75
- shift_one: bfloat16 [1024], replicated, may hold values from -2 to 2
- gain_two: bfloat16 [1024], replicated, may hold values from 0.25 to 1.75
- shift_two: bfloat16 [1024], replicated, may hold values from -2 to 2
Outputs:
- layer_out: bfloat16 [16384, 1024], P(('dp', 'seq'))
- grad_tokens: bfloat16 [16384, 1024], P(('dp', 'seq'))
- grad_w_query: float32 [1024, 1024], P('seq')
- grad_w_key: float32 [1024, 1024], P('seq')
- grad_w_value: float32 [1024, 1024], P('seq')
- grad_w_out: float32 [1024, 1024], P('seq')
- grad_w_time: float32 [1024, 1024], P('seq')
- grad_w_in: float32 [4096, 1024], P('seq')
- grad_w_down: float32 [4096, 1024], P('seq')
- grad_b_query: float32 [1024], replicated
- grad_b_value: float32 [1024], replicated
- grad_b_out: float32 [1024], replicated
- grad_b_time: float32 [1024], replicated
- grad_b_in: float32 [4096], replicated
- grad_b_down: float32 [1024], replicated
- grad_gain_one: float32 [1024], replicated
- grad_shift_one: float32 [1024], replicated
- grad_gain_two: float32 [1024], replicated
- grad_shift_two: float32 [1024], replicated
Inputs may be any that keep to these rules, and one draw needn't show every extreme that they name: Item i's valid slots are its first lengths[i] + 25; every draw has an item of length 475 and one of length 0.
All inputs are finite; a program needn't handle non-finite values.
Results may differ from a plain program's by a relative error of at most 0.02.
Values may be sent and summed in bfloat16 or wider, within the bound.
A program may use at most 256 MiB of HBM per device.

v0:
```python
import jax
import jax.numpy as jnp
from jax import lax
from jax.sharding import PartitionSpec as P

HEAD_DIM = 64
BLOCK = 25
norm_eps = 1e-05
neg_large = -1e30


def layer_norm(values, gain, shift):
    center = values - jnp.mean(values, axis=-1, keepdims=True)
    spread = lax.rsqrt(jnp.mean(center * center, axis=-1, keepdims=True) + norm_eps)
    return center * spread * gain + shift


def exact_gelu(values):
    return jax.nn.gelu(values, approximate=False)


def split_heads(rows):
    return rows.reshape(rows.shape[0], rows.shape[1] // HEAD_DIM, HEAD_DIM)


def item_scores(queries, keys, key_valid):
    scores = jnp.einsum(
        "qhd,khd->hqk", split_heads(queries), split_heads(keys), preferred_element_type=jnp.float32
    ) * HEAD_DIM ** (-0.5)
    return jnp.where(key_valid[None, None, :], scores, neg_large)


def attend_forward(queries, keys, values, key_valid):
    masked = item_scores(queries, keys, key_valid)
    row_max = jnp.max(masked, axis=-1, keepdims=True)
    exp_scores = jnp.exp(masked - row_max)
    row_total = jnp.sum(exp_scores, axis=-1, keepdims=True)
    soft = (exp_scores / row_total).astype(jnp.bfloat16)
    mixed = jnp.einsum(
        "hqk,khd->qhd", soft, split_heads(values), preferred_element_type=jnp.float32
    )
    log_total = row_max[:, :, 0] + jnp.log(row_total[:, :, 0])
    return (mixed.reshape(queries.shape).astype(jnp.bfloat16), log_total)


def attend_backward(queries, keys, values, key_valid, log_total, grad_mixed):
    masked = item_scores(queries, keys, key_valid)
    soft = jnp.exp(masked - log_total[:, :, None])
    grad_heads = split_heads(grad_mixed)
    grad_value = jnp.einsum(
        "hqk,qhd->khd", soft.astype(jnp.bfloat16), grad_heads, preferred_element_type=jnp.float32
    )
    grad_soft = jnp.einsum(
        "qhd,khd->hqk", grad_heads, split_heads(values), preferred_element_type=jnp.float32
    )
    grad_scores = soft * (grad_soft - jnp.sum(soft * grad_soft, axis=-1, keepdims=True))
    scores_low = grad_scores.astype(jnp.bfloat16)
    scale = HEAD_DIM ** (-0.5)
    grad_query = scale * jnp.einsum(
        "hqk,khd->qhd", scores_low, split_heads(keys), preferred_element_type=jnp.float32
    )
    grad_key = scale * jnp.einsum(
        "hqk,qhd->khd", scores_low, split_heads(queries), preferred_element_type=jnp.float32
    )
    return tuple(
        (
            grad.reshape(queries.shape).astype(jnp.bfloat16)
            for grad in (grad_query, grad_key, grad_value)
        )
    )


def per_item(fn, item_count, slot_count, *arrays):
    if item_count == 1:
        return fn(*[a[0] for a in arrays])
    outs = lax.map(lambda packed: fn(*packed), arrays)
    return outs


def local(
    tokens,
    time_embed,
    lengths,
    cotangent,
    w_query,
    w_key,
    w_value,
    w_out,
    w_time,
    w_in,
    w_down,
    b_query,
    b_value,
    b_out,
    b_time,
    b_in,
    b_down,
    gain_one,
    shift_one,
    gain_two,
    shift_two,
):
    f32, bf16 = (jnp.float32, jnp.bfloat16)
    seq_rank = lax.axis_index("seq")
    item_count = time_embed.shape[0]
    token_count = tokens.shape[0]
    slot_count = token_count // item_count
    width = tokens.shape[1]
    rows = w_time.shape[0]

    def mm(a, b, dims):
        return lax.dot_general(a, b, (dims, ((), ())), preferred_element_type=f32)

    def gather(a):
        return lax.all_gather(a, "seq", axis=0, tiled=True)

    def scatter_sum(a):
        return lax.psum_scatter(a, "seq", scatter_dimension=0, tiled=True)

    full_time, full_query, full_key, full_value, full_out = (
        gather(w_time),
        gather(w_query),
        gather(w_key),
        gather(w_value),
        gather(w_out),
    )
    own_lengths = lax.dynamic_slice_in_dim(lengths, seq_rank * item_count, item_count, 0)
    slot_index = lax.broadcasted_iota(jnp.int32, (item_count, slot_count), 1)
    own_valid = slot_index < own_lengths[:, None] + BLOCK
    row_keep = own_valid.reshape(token_count, 1).astype(f32)
    time_proj = mm(time_embed, full_time, ((1,), (0,))) + b_time.astype(f32)
    resid = (tokens.reshape(item_count, slot_count, width) + time_proj[:, None, :]).reshape(
        token_count, width
    )
    resid_low = resid.astype(bf16)
    query_rows = (mm(resid_low, full_query, ((1,), (0,))) + b_query.astype(f32)).astype(bf16)
    key_rows = mm(resid_low, full_key, ((1,), (0,))).astype(bf16)
    value_rows = (mm(resid_low, full_value, ((1,), (0,))) + b_value.astype(f32)).astype(bf16)

    def split_items(a):
        return a.reshape(item_count, slot_count, -1)

    qkv = [split_items(a) for a in (query_rows, key_rows, value_rows)]
    mixed, log_total = per_item(attend_forward, item_count, slot_count, *qkv, own_valid)
    mixed_rows = mixed.reshape(token_count, width)
    attn_out = mm(mixed_rows, full_out, ((1,), (0,))) + b_out.astype(f32)
    first_norm, first_pull = jax.vjp(
        layer_norm, resid + attn_out, gain_one.astype(f32), shift_one.astype(f32)
    )
    first_group = gather(first_norm.astype(bf16))
    bias_in = lax.dynamic_slice_in_dim(b_in, seq_rank * w_in.shape[0], w_in.shape[0], 0)
    hidden_pre = mm(first_group, w_in, ((1,), (1,))) + bias_in.astype(f32)
    hidden, gelu_pull = jax.vjp(exact_gelu, hidden_pre)
    hidden_low = hidden.astype(bf16)
    ffn_part = mm(hidden_low, w_down, ((1,), (0,))).astype(bf16)
    ffn_out = scatter_sum(ffn_part).astype(f32) + b_down.astype(f32)
    second_norm, second_pull = jax.vjp(
        layer_norm, first_norm + ffn_out, gain_two.astype(f32), shift_two.astype(f32)
    )
    layer_out = (second_norm * row_keep).astype(bf16)
    grad_second_in, grad_gain_two, grad_shift_two = second_pull(cotangent.astype(f32) * row_keep)
    grad_ffn = grad_second_in.astype(bf16)
    grad_group = gather(grad_ffn)
    grad_hidden = mm(grad_group, w_down, ((1,), (1,)))
    grad_pre = gelu_pull(grad_hidden)[0].astype(bf16)
    back_part = mm(grad_pre, w_in, ((1,), (0,))).astype(bf16)
    grad_first = grad_second_in + scatter_sum(back_part).astype(f32)
    term_in = mm(grad_pre, first_group, ((0,), (0,))).astype(bf16)
    term_down = mm(hidden_low, grad_group, ((0,), (0,))).astype(bf16)
    sum_ffn = lax.psum(jnp.concatenate([term_in, term_down], axis=0), "dp").astype(f32)
    grad_first_in, grad_gain_one, grad_shift_one = first_pull(grad_first)
    grad_attn = grad_first_in.astype(bf16)
    grad_mixed = mm(grad_attn, full_out, ((1,), (1,))).astype(bf16)
    if item_count == 1:
        extra = (log_total[None], split_items(grad_mixed))
    else:
        extra = (log_total, split_items(grad_mixed))
    grad_query, grad_key, grad_value = (
        a.reshape(token_count, width)
        for a in per_item(attend_backward, item_count, slot_count, *qkv, own_valid, *extra)
    )
    grad_resid = (
        grad_first_in
        + mm(grad_query, full_query, ((1,), (1,)))
        + mm(grad_key, full_key, ((1,), (1,)))
        + mm(grad_value, full_value, ((1,), (1,)))
    )
    grad_tokens = grad_resid.astype(bf16)
    grad_time = jnp.sum(grad_resid.reshape(item_count, slot_count, width), axis=1).astype(bf16)
    terms = [
        mm(resid_low, grad_query, ((0,), (0,))),
        mm(resid_low, grad_key, ((0,), (0,))),
        mm(resid_low, grad_value, ((0,), (0,))),
        mm(mixed_rows, grad_attn, ((0,), (0,))),
    ]
    group = w_out.shape[0]
    stacked = jnp.stack([t.astype(bf16).reshape(-1, group, width) for t in terms], axis=1)
    share = scatter_sum(stacked.reshape(-1, width))
    sum_attn = lax.psum(share, "dp").astype(f32)
    small = jnp.concatenate(
        [
            jnp.stack(
                [
                    jnp.sum(grad_query, axis=0, dtype=f32),
                    jnp.sum(grad_value, axis=0, dtype=f32),
                    jnp.sum(grad_attn, axis=0, dtype=f32),
                    jnp.sum(grad_ffn, axis=0, dtype=f32),
                    grad_gain_one,
                    grad_shift_one,
                    grad_gain_two,
                    grad_shift_two,
                ]
            ).astype(bf16),
            jnp.sum(grad_pre, axis=0, dtype=f32).reshape(-1, width).astype(bf16),
            time_embed,
            grad_time,
        ],
        axis=0,
    )
    every = lax.all_gather(small, ("dp", "seq"), axis=0)
    vectors = jnp.sum(every[:, :8], axis=0, dtype=f32)
    hidden_rows = every.shape[1] - 8 - 2 * item_count
    in_parts = every[:, 8 : 8 + hidden_rows].reshape(-1, b_in.shape[0])
    grad_b_in = jnp.sum(in_parts, axis=0, dtype=f32)
    time_rows = every[:, 8 + hidden_rows : 8 + hidden_rows + item_count].reshape(-1, width)
    time_grads = every[:, 8 + hidden_rows + item_count :].reshape(-1, width)
    own_columns = lax.dynamic_slice_in_dim(time_rows, seq_rank * rows, rows, 1)
    grad_w_time = mm(own_columns, time_grads, ((0,), (0,)))
    grad_b_time = jnp.sum(time_grads, axis=0, dtype=f32)
    return (
        layer_out,
        grad_tokens,
        sum_attn[:group],
        sum_attn[group : 2 * group],
        sum_attn[2 * group : 3 * group],
        sum_attn[3 * group :],
        grad_w_time,
        sum_ffn[: w_in.shape[0]],
        sum_ffn[w_in.shape[0] :],
        vectors[0],
        vectors[1],
        vectors[2],
        grad_b_time,
        grad_b_in,
        vectors[3],
        vectors[4],
        vectors[5],
        vectors[6],
        vectors[7],
    )


def solution(mesh):
    in_specs = (
        P(("dp", "seq"), None),
        P(("dp", "seq"), None),
        P("dp"),
        P(("dp", "seq"), None),
        P("seq", None),
        P("seq", None),
        P("seq", None),
        P("seq", None),
        P("seq", None),
        P("seq", None),
        P("seq", None),
        P(),
        P(),
        P(),
        P(),
        P(),
        P(),
        P(),
        P(),
        P(),
        P(),
    )
    out_specs = (
        P(("dp", "seq"), None),
        P(("dp", "seq"), None),
        P("seq", None),
        P("seq", None),
        P("seq", None),
        P("seq", None),
        P("seq", None),
        P("seq", None),
        P("seq", None),
        P(),
        P(),
        P(),
        P(),
        P(),
        P(),
        P(),
        P(),
        P(),
        P(),
    )
    return jax.shard_map(local, mesh=mesh, in_specs=in_specs, out_specs=out_specs, check_vma=False)
```

profile of v0, /device:TPU:0, one launch (start us, length us, event | category | flops | bytes accessed | tf_op | source)
XLA Modules:
  0.0 732.2 jit_solution(3286179977434555433)
XLA Ops:
  16.0 18.9 %all-gather.10.cloned.1.call-done = bf16[1024,1024]{1,0:T(8,128)(2,1)} async-done(((bf16[256,1024]{1,0:T(8,128)(2,1)}), bf16[1024,1024]{1,0:T(8,128)(2,1)}) %all-gather.10.cloned.1.call-update) | async-done | bytes 2097168 | tf_op jit(solution)/shard_map/all_gather | solution.py:115
  36.9 22.1 %all-gather.14.cloned.1.call-done = bf16[1024,1024]{1,0:T(8,128)(2,1)} async-done(((bf16[256,1024]{1,0:T(8,128)(2,1)}), bf16[1024,1024]{1,0:T(8,128)(2,1)}) %all-gather.14.cloned.1.call-update) | async-done | bytes 2097168 | tf_op jit(solution)/shard_map/all_gather | solution.py:115
  59.1 3.2 add_convert_fusion.1
  63.6 19.7 %all-gather.16.cloned.1.call-done = bf16[1024,1024]{1,0:T(8,128)(2,1)} async-done(((bf16[256,1024]{1,0:T(8,128)(2,1)}), bf16[1024,1024]{1,0:T(8,128)(2,1)}) %all-gather.16.cloned.1.call-update) | async-done | bytes 2097168 | tf_op jit(solution)/shard_map/all_gather | solution.py:115
  83.2 4.1 convolution_convert_fusion.9
  88.9 9.2 %fusion.46 = (f32[16,512]{1,0:T(8,128)S(1)}, f32[16,512,512]{1,2,0:T(8,128)}) fusion(bf16[512,16,64]{0,2,1:T(8,128)(2,1)} %bitcast.89, bf16[512,16,64]{0,2,1:T(8,128)(2,1)S(1)} %bitcast.87, pred[512]{0:T(512)(128)(4,1)S(1)} %iota_compare_fusion), kind=kOutput, calls=%fused_computation.107 | convolution fusion | flops 549445632 | bytes 18907648 | tf_op jit(solution)/shard_map/qhd,khd->hqk/dot_general | solution.py:27
  98.0 9.2 %all-gather.12.cloned.1.call-done = bf16[1024,1024]{1,0:T(8,128)(2,1)} async-done(((bf16[256,1024]{1,0:T(8,128)(2,1)}), bf16[1024,1024]{1,0:T(8,128)(2,1)}) %all-gather.12.cloned.1.call-update) | async-done | bytes 2097168 | tf_op jit(solution)/shard_map/all_gather | solution.py:115
  107.2 4.1 add_convert_fusion.2
  112.9 9.4 %fusion = f32[16,512]{1,0:T(8,128)S(1)} fusion(f32[16,512,512]{1,2,0:T(8,128)} %get-tuple-element.61, f32[16,512]{1,0:T(8,128)S(1)} %get-tuple-element.60), kind=kLoop, calls=%fused_computation.6 | loop fusion | flops 8380416 | bytes 16842752 | tf_op jit(solution)/shard_map/reduce_sum | solution.py:37
  122.2 8.5 %fusion.16 = bf16[16,64,512]{2,1,0:T(8,128)(2,1)} fusion(bf16[512,16,64]{0,2,1:T(8,128)(2,1)S(1)} %bitcast.93, f32[16,512,512]{1,2,0:T(8,128)} %get-tuple-element.61, f32[16,512]{1,0:T(8,128)S(1)} %fusion, f32[16,512]{1,0:T(8,128)S(1)} %get-tuple-element.60), kind=kOutput, calls=%fused_computation.64 | convolution fusion | flops 549978112 | bytes 18939904 | tf_op jit(solution)/shard_map/hqk,khd->qhd/dot_general | solution.py:39
  131.2 3.6 fusion.47
  138.5 33.7 %all-gather.20.cloned.1.call-done = bf16[2048,1024]{1,0:T(8,128)(2,1)} async-done(((bf16[512,1024]{1,0:T(8,128)(2,1)}), bf16[2048,1024]{1,0:T(8,128)(2,1)}) %all-gather.20.cloned.1.call-update) | async-done | bytes 4194320 | tf_op jit(solution)/shard_map/all_gather | solution.py:115
  172.1 25.7 %multiply_convert_fusion.1 = (bf16[2048,1024]{1,0:T(8,128)(2,1)S(1)}, f32[2048,1024]{1,0:T(8,128)}, f32[2048,1024]{1,0:T(8,128)}) fusion(f32[1024]{0:T(1024)S(1)} %dynamic-slice_convert_fusion, bf16[2048,1024]{1,0:T(8,128)(2,1)} %all-gather.20.cloned.1.call-done, bf16[1024,1024]{1,0:T(8,128)(2,1)S(1)} %copy-done), kind=kOutput, calls=%fused_computation.14 | convolution fusion | flops 4433379328 | bytes 27267072 | tf_op jit(solution)/shard_map/dot_general | solution.py:112
  199.8 6.0 convolution_convert_fusion.1
  206.6 44.0 %reduce-scatter.4.cloned.1.call-done = bf16[512,1024]{1,0:T(8,128)(2,1)} async-done(((bf16[2048,1024]{1,0:T(8,128)(2,1)}), bf16[512,1024]{1,0:T(8,128)(2,1)}) %reduce-scatter.4.cloned.1.call-update) | async-done | bytes 1048592 | tf_op jit(solution)/shard_map/reduce_scatter | solution.py:118
  259.6 34.2 %all-gather.22.cloned.1.call-done = bf16[2048,1024]{1,0:T(8,128)(2,1)} async-done(((bf16[512,1024]{1,0:T(8,128)(2,1)}), bf16[2048,1024]{1,0:T(8,128)(2,1)}) %all-gather.22.cloned.1.call-update) | async-done | bytes 4194320 | tf_op jit(solution)/shard_map/all_gather | solution.py:115
  293.8 13.3 %fusion.34 = (bf16[1024]{0:T(1024)(128)(2,1)S(1)}, bf16[2048,1024]{1,0:T(8,128)(2,1)S(1)}) fusion(f32[2048,1024]{1,0:T(8,128)} %get-tuple-element.40, f32[2048,1024]{1,0:T(8,128)} %get-tuple-element.64, f32[1024]{0:T(1024)S(1)} %dynamic-slice_convert_fusion, bf16[2048,1024]{1,0:T(8,128)(2,1)} %all-gather.22.cloned.1.call-done, bf16[1024,1024]{1,0:T(8,128)(2,1)} %param.31), kind=kOutput, calls=%fused_computation.96 | convolution fusion | flops 4328520704 | bytes 27269120 | tf_op jit(solution)/shard_map/dot_general | solution.py:112
  309.1 6.0 convolution_convert_fusion
  315.2 44.7 %reduce-scatter.6.cloned.1.call-done = bf16[512,1024]{1,0:T(8,128)(2,1)} async-done(((bf16[2048,1024]{1,0:T(8,128)(2,1)}), bf16[512,1024]{1,0:T(8,128)(2,1)}) %reduce-scatter.6.cloned.1.call-update) | async-done | bytes 1048592 | tf_op jit(solution)/shard_map/reduce_scatter | solution.py:118
  359.8 3.7 multiply_reduce_fusion.2
  370.2 11.4 %multiply_reduce_fusion = (f32[16,512]{1,0:T(8,128)S(1)}, f32[16,512,512]{1,2,0:T(8,128)}) fusion(f32[16,512,512]{1,2,0:T(8,128)} %get-tuple-element.61, f32[16,512]{1,0:T(8,128)S(1)} %log_add_fusion, bf16[512,16,64]{0,2,1:T(8,128)(2,1)S(1)} %bitcast.91, bf16[512,16,64]{0,2,1:T(8,128)(2,1)} %bitcast.94), kind=kOutput, calls=%fused_computation.1 | convolution fusion | flops 549445632 | bytes 35717120 | tf_op jit(solution)/shard_map/qhd,khd->hqk/dot_general | solution.py:53
  381.6 12.0 %multiply_convert_fusion = bf16[16,512,512]{1,2,0:T(8,128)(2,1)S(1)} fusion(f32[16,512,512]{1,2,0:T(8,128)} %get-tuple-element.66, f32[16,512,512]{1,2,0:T(8,128)} %get-tuple-element.61, f32[16,512]{1,0:T(8,128)S(1)} %get-tuple-element.65, f32[16,512]{1,0:T(8,128)S(1)} %log_add_fusion), kind=kLoop, calls=%fused_computation | loop fusion | flops 16777216 | bytes 42008576 | tf_op jit(solution)/shard_map/convert_element_type | solution.py:57
  399.1 8.6 %bitcast_reduce_fusion = (bf16[16,64]{1,0:T(8,128)(2,1)S(1)}, bf16[16,64,512]{2,1,0:T(8,128)(2,1)S(1)}) fusion(bf16[512,16,64]{0,2,1:T(8,128)(2,1)S(1)} %bitcast.92, f32[16,512,512]{1,2,0:T(8,128)} %get-tuple-element.61, f32[16,512]{1,0:T(8,128)S(1)} %log_add_fusion), kind=kOutput, calls=%fused_computation.68 | convolution fusion | flops 546307072 | bytes 18909184 | tf_op jit(solution)/shard_map/hqk,qhd->khd/dot_general | solution.py:50
  411.8 3.8 pad_maximum_fusion
  415.6 7.9 %copy.79 = bf16[4,4,256,1024]{3,2,1,0:T(8,128)(2,1)} copy(bf16[4,4,256,1024]{3,2,0,1:T(8,128)(2,1)} %pad_maximum_fusion) | data formatting | bytes 16777216 | tf_op jit(solution)/shard_map/stack | solution.py:197
  423.9 8.2 %convolution_convert_fusion.2 = bf16[1024,1024]{1,0:T(8,128)(2,1)S(1)} fusion(bf16[2048,1024]{1,0:T(8,128)(2,1)} %copy-done.36, bf16[2048,1024]{1,0:T(8,128)(2,1)} %all-gather.22.cloned.1.call-done), kind=kOutput, calls=%fused_computation.57 | convolution fusion | flops 4296015872 | bytes 10485760 | tf_op jit(solution)/shard_map/dot_general | solution.py:112
  432.1 4.8 convolution_convert_fusion.3
  439.3 55.8 %reduce-scatter.8.cloned.1.call-done = bf16[1024,1024]{1,0:T(8,128)(2,1)} async-done(((bf16[4096,1024]{1,0:T(8,128)(2,1)}), bf16[1024,1024]{1,0:T(8,128)(2,1)}) %reduce-scatter.8.cloned.1.call-update) | async-done | bytes 2097168 | tf_op jit(solution)/shard_map/reduce_scatter | solution.py:118
  495.2 3.0 fusion.48
  503.7 51.7 %all-gather.1 = bf16[32,11,1024]{2,1,0:T(8,128)(2,1)S(1)} all-gather(bf16[1,11,1024]{2,1,0:T(8,128)(2,1)S(1)} %bitcast.107), channel_id=2, replica_groups=mesh['dp'=8,'seq'=4] {'dp','seq'}, dimensions={0}, use_global_device_ids=true | all-gather | bytes 743424 | tf_op jit(solution)/shard_map/all_gather | solution.py:220
  559.3 156.8 %all-reduce.3.cloned.1.call-done = (bf16[1024,1024]{1,0:T(8,128)(2,1)}, bf16[2048,1024]{1,0:T(8,128)(2,1)}) async-done(((bf16[1024,1024]{1,0:T(8,128)(2,1)}, bf16[2048,1024]{1,0:T(8,128)(2,1)}), (bf16[1024,1024]{1,0:T(8,128)(2,1)}, bf16[2048,1024]{1,0:T(8,128)(2,1)})) %all-reduce.3.cloned.1.call-update) | async-done | bytes 6291472 | tf_op jit(solution)/shard_map/psum | solution.py:199
  716.2 6.8 fusion.41
  (168 shorter events, 62.5 us)
Async XLA Ops:
  7.2 164.9 %copy-start = (bf16[1024,1024]{1,0:T(8,128)(2,1)S(1)}, bf16[1024,1024]{1,0:T(8,128)(2,1)}, u32[]{:S(2)}) copy-start(bf16[1024,1024]{1,0:T(8,128)(2,1)} %param.30) | copy-start | bytes 6291460
  7.2 29.7 %copy-start.28 = (bf16[1024]{0:T(1024)(128)(2,1)S(1)}, bf16[1024]{0:T(1024)(128)(2,1)}, u32[]{:S(2)}) copy-start(bf16[1024]{0:T(1024)(128)(2,1)} %param.35) | copy-start | bytes 6148
  7.2 27.7 %all-gather.10.cloned.1.call-start = ((), (), s32[]{:S(2)}) async-start(), calls=%async_computation.3 | async-start | bytes 2621440 | tf_op jit(solution)/shard_map/all_gather | solution.py:115
  7.9 51.1 %all-gather.14.cloned.1.call-start = ((), (), s32[]{:S(2)}) async-start(), calls=%async_computation.5 | async-start | bytes 2621440 | tf_op jit(solution)/shard_map/all_gather | solution.py:115
  8.7 74.5 %all-gather.16.cloned.1.call-start = ((), (), s32[]{:S(2)}) async-start(), calls=%async_computation.6 | async-start | bytes 2621440 | tf_op jit(solution)/shard_map/all_gather | solution.py:115
  9.4 97.8 %all-gather.12.cloned.1.call-start = ((), (), s32[]{:S(2)}) async-start(), calls=%async_computation.4 | async-start | bytes 2621440 | tf_op jit(solution)/shard_map/all_gather | solution.py:115
  10.0 121.2 %all-gather.18.cloned.1.call-start = ((), (), s32[]{:S(2)}) async-start(), calls=%async_computation.7 | async-start | bytes 2621440 | tf_op jit(solution)/shard_map/all_gather | solution.py:115
  10.6 161.5 %all-gather.20.cloned.1.call-start = ((), (), s32[]{:S(2)}) async-start(), calls=%async_computation.8 | async-start | bytes 5242880 | tf_op jit(solution)/shard_map/all_gather | solution.py:115
  36.9 94.3 %copy-start.25 = (f32[1024]{0:T(1024)}, f32[1024]{0:T(1024)S(1)}, u32[]{:S(2)}) copy-start(f32[1024]{0:T(1024)S(1)} %convert_add_fusion.2) | copy-start | bytes 12292
  88.9 9.2 %copy-start.5 = (bf16[512,1024]{0,1:T(8,128)(2,1)}, bf16[512,1024]{0,1:T(8,128)(2,1)S(1)}, u32[]{:S(2)}) copy-start(bf16[512,1024]{0,1:T(8,128)(2,1)S(1)} %copy.73) | copy-start | bytes 3145732
  112.9 9.4 %copy-start.11 = (bf16[512,1024]{0,1:T(8,128)(2,1)}, bf16[512,1024]{0,1:T(8,128)(2,1)S(1)}, u32[]{:S(2)}) copy-start(bf16[512,1024]{0,1:T(8,128)(2,1)S(1)} %copy.71) | copy-start | bytes 3145732
  137.5 113.1 %reduce-scatter.4.cloned.1.call-start = ((), (), s32[]{:S(2)}) async-start(), calls=%async_computation.9 | async-start | bytes 5242880 | tf_op jit(solution)/shard_map/reduce_scatter | solution.py:118
  172.1 27.7 %copy-start.33 = (bf16[1024,1024]{1,0:T(8,128)(2,1)S(1)}, bf16[1024,1024]{1,0:T(8,128)(2,1)}, u32[]{:S(2)}) copy-start(bf16[1024,1024]{1,0:T(8,128)(2,1)} %param.31) | copy-start | bytes 6291460
  205.9 47.8 %copy-start.12 = (bf16[512,1024]{1,0:T(8,128)(2,1)S(1)}, bf16[512,1024]{1,0:T(8,128)(2,1)}, u32[]{:S(2)}) copy-start(bf16[512,1024]{1,0:T(8,128)(2,1)} %param.24) | copy-start | bytes 3145732
  205.9 87.9 %all-gather.22.cloned.1.call-start = ((), (), s32[]{:S(2)}) async-start(), calls=%async_computation.10 | async-start | bytes 5242880 | tf_op jit(solution)/shard_map/all_gather | solution.py:115
  259.2 100.6 %reduce-scatter.6.cloned.1.call-start = ((), (), s32[]{:S(2)}) async-start(), calls=%async_computation.11 | async-start | bytes 5242880 | tf_op jit(solution)/shard_map/reduce_scatter | solution.py:118
  315.1 180.0 %reduce-scatter.8.cloned.1.call-start = ((), (), s32[]{:S(2)}) async-start(), calls=%async_computation.12 | async-start | bytes 10485760 | tf_op jit(solution)/shard_map/reduce_scatter | solution.py:118
  359.8 3.7 copy-start.2
  359.8 3.8 copy-start.4
  359.8 4.0 copy-start.13
  381.6 12.0 %copy-start.6 = (bf16[512,1024]{0,1:T(8,128)(2,1)S(1)}, bf16[512,1024]{0,1:T(8,128)(2,1)}, u32[]{:S(2)}) copy-start(bf16[512,1024]{0,1:T(8,128)(2,1)} %copy-done.5) | copy-start | bytes 3145732
  395.2 12.6 %copy-start.14 = (bf16[16,64,512]{2,1,0:T(8,128)(2,1)}, bf16[16,64,512]{2,1,0:T(8,128)(2,1)S(1)}, u32[]{:S(2)}) copy-start(bf16[16,64,512]{2,1,0:T(8,128)(2,1)S(1)} %get-tuple-element.69) | copy-start | bytes 3145732
  397.8 11.3 %copy-start.17 = (bf16[16,64,512]{2,1,0:T(8,128)(2,1)}, bf16[16,64,512]{2,1,0:T(8,128)(2,1)S(1)}, u32[]{:S(2)}) copy-start(bf16[16,64,512]{2,1,0:T(8,128)(2,1)S(1)} %multiply_convert_fusion.2) | copy-start | bytes 3145732
  399.1 8.7 %copy-start.21 = (bf16[512,1024]{1,0:T(8,128)(2,1)S(1)}, bf16[512,1024]{1,0:T(8,128)(2,1)}, u32[]{:S(2)}) copy-start(bf16[512,1024]{1,0:T(8,128)(2,1)} %param.21) | copy-start | bytes 3145732
  399.1 8.7 %copy-start.26 = (f32[1024]{0:T(1024)S(1)}, f32[1024]{0:T(1024)}, u32[]{:S(2)}) copy-start(f32[1024]{0:T(1024)} %copy-done.25) | copy-start | bytes 12292
  423.6 292.6 %all-reduce.3.cloned.1.call-start = ((), (), s32[]{:S(2)}) async-start(), calls=%async_computation.13 | async-start | bytes 12582912 | tf_op jit(solution)/shard_map/psum | solution.py:199
  423.8 8.2 %copy-start.32 = (bf16[2048,1024]{1,0:T(8,128)(2,1)S(1)}, bf16[2048,1024]{1,0:T(8,128)(2,1)}, u32[]{:S(2)}) copy-start(bf16[2048,1024]{1,0:T(8,128)(2,1)} %all-gather.20.cloned.1.call-done) | copy-start | bytes 12582916
  423.8 8.2 %copy-start.38 = (bf16[2048,1024]{1,0:T(8,128)(2,1)S(1)}, bf16[2048,1024]{1,0:T(8,128)(2,1)}, u32[]{:S(2)}) copy-start(bf16[2048,1024]{1,0:T(8,128)(2,1)} %copy-done.37) | copy-start | bytes 12582916
  439.3 55.9 %copy-start.15 = (bf16[16,64,512]{2,1,0:T(8,128)(2,1)S(1)}, bf16[16,64,512]{2,1,0:T(8,128)(2,1)}, u32[]{:S(2)}) copy-start(bf16[16,64,512]{2,1,0:T(8,128)(2,1)} %copy-done.14) | copy-start | bytes 3145732
  495.2 3.1 copy-start.18
  495.2 3.1 copy-start.34
  716.2 6.8 copy-start.10
  (18 other events, 32.2 us)
Sparse Core Ops, SparseCore 0:
  9.6 25.2 all-gather.9
  36.5 22.5 all-gather.13
  60.6 22.5 all-gather.15
  84.6 22.5 all-gather.11
  108.6 22.5 all-gather.17
  137.6 34.4 all-gather.19
  206.0 44.5 reduce-scatter.3
  259.3 34.4 all-gather.21
  315.2 44.5 reduce-scatter.5
  423.7 71.3 reduce-scatter.7
  499.6 216.4 all-reduce.2
where the time goes:
time: 741 us; the launch traced here: 732 us
  waiting for transfers between devices  443 us (60%)
  matrix products  138 us (19%)
  blocking collectives  51.7 us (7%)
  other arithmetic  47.2 us (6%)
  local copies, waits for them, and re-layouts  35.2 us (5%)
  between operations  15.6 us (2%)
    psum x1, waiting for transfers between devices, local(): sum_attn = lax.psum(share, 'dp').astype(f32)  157 us
    reduce_scatter x3, waiting for transfers between devices, scatter_sum(): return lax.psum_scatter(a, 'seq', scatter_dimension=0, tiled=True)  145 us
    all_gather x7, waiting for transfers between devices, gather(): return lax.all_gather(a, 'seq', axis=0, tiled=True)  138 us
    dot_general x20, matrix products, mm(): return lax.dot_general(a, b, (dims, ((), ())), preferred_element_type=f32)  96.6 us
    all_gather x1, blocking collectives, local(): every = lax.all_gather(small, ('dp', 'seq'), axis=0)  51.7 us
  transfers between devices with their start and end apart: 11, of which 11 were waited for; matrix products, arithmetic and copies ran while one was open for 10% of the time, Pallas kernels for 0%

commit v1 on v0

--- a/solution.py
+++ b/solution.py
@@ -7,6 +7,27 @@
 BLOCK = 25
 norm_eps = 1e-05
 neg_large = -1e30
+
+
+def convert_state_in(xin):
+    current_arr = lax.axis_size("seq")
+    passed, formed, raw_out = (current_arr, lax.axis_index("seq"), xin.shape[0])
+    low, outcome_arr = (xin, 1)
+    while outcome_arr < passed:
+        low = jnp.concatenate(
+            [
+                low,
+                lax.ppermute(
+                    low,
+                    "seq",
+                    list(map(lambda kk: (kk, (kk - outcome_arr) % passed), range(passed))),
+                ),
+            ],
+            axis=0,
+        )
+        outcome_arr = 2 * outcome_arr
+    response = jnp.roll(low, formed * raw_out, axis=0)
+    return response
 
 
 def layer_norm(values, gain, shift):
@@ -112,7 +133,7 @@
         return lax.dot_general(a, b, (dims, ((), ())), preferred_element_type=f32)
 
     def gather(a):
-        return lax.all_gather(a, "seq", axis=0, tiled=True)
+        return convert_state_in(a)
 
     def scatter_sum(a):
         return lax.psum_scatter(a, "seq", scatter_dimension=0, tiled=True)

time: 741 us -> 888 us (1.20)
  waiting for transfers between devices: 443 us -> 513 us
  other arithmetic: 47.2 us -> 113 us
  starting transfers between devices: 1.27 us -> 12.5 us
    ppermute x0 -> x14, waiting for transfers between devices: none -> 209 us  [convert_state_in(): lax.ppermute(low, 'seq', list(map(lambda kk: (kk, (kk - outcome_arr) % pa...]
    all_gather x7 -> x0, waiting for transfers between devices: 138 us -> none  [gather(): return lax.all_gather(a, 'seq', axis=0, tiled=True)]
    concatenate x0 -> x13, other arithmetic: none -> 68.3 us  [the longest x6 56.9 us: convert_state_in(): response = jnp.roll(low, formed * raw_out, axis=0)]
    ppermute x0 -> x14, starting transfers between devices: none -> 12.1 us  [convert_state_in(): lax.ppermute(low, 'seq', list(map(lambda kk: (kk, (kk - outcome_arr) % pa...]
  transfers between devices with their start and end apart: 11 -> 18, of which waited for: 11 -> 14; matrix products, arithmetic and copies ran while one was open for 10% -> 12% of each run, Pallas kernels for 0% -> 0%
where the time goes in v1:
time: 888 us; the launch traced here: 879 us
  waiting for transfers between devices  513 us (58%)
  matrix products  132 us (15%)
  other arithmetic  113 us (13%)
  blocking collectives  51.5 us (6%)
  local copies, waits for them, and re-layouts  41.4 us (5%)
  between operations  15.7 us (2%)
  starting transfers between devices  12.5 us (1%)
    ppermute x14, waiting for transfers between devices, convert_state_in(): lax.ppermute(low, 'seq', list(map(lambda kk: (kk, (kk - outcome_arr) % pa...  209 us
    psum x1, waiting for transfers between devices, local(): sum_attn = lax.psum(share, 'dp').astype(f32)  157 us
    reduce_scatter x3, waiting for transfers between devices, scatter_sum(): return lax.psum_scatter(a, 'seq', scatter_dimension=0, tiled=True)  148 us
    dot_general x20, matrix products, mm(): return lax.dot_general(a, b, (dims, ((), ())), preferred_element_type=f32)  90.6 us
    concatenate x6, other arithmetic, convert_state_in(): response = jnp.roll(low, formed * raw_out, axis=0)  56.9 us
    all_gather x1, blocking collectives, local(): every = lax.all_gather(small, ('dp', 'seq'), axis=0)  51.5 us
  transfers between devices with their start and end apart: 18, of which 14 were waited for; matrix products, arithmetic and copies ran while one was open for 12% of the time, Pallas kernels for 0%

profile of v1, /device:TPU:0, one launch (start us, length us, event | category | flops | bytes accessed | tf_op | source)
XLA Modules:
  0.0 878.6 jit_solution(17638638668347512443)
XLA Ops:
  10.4 6.3 collective-permute-done
  30.7 25.5 %collective-permute-done.6 = bf16[256,1024]{1,0:T(8,128)(2,1)} collective-permute-done((bf16[256,1024]{1,0:T(8,128)(2,1)}, bf16[256,1024]{1,0:T(8,128)(2,1)}, u32[]{:S(2)}, u32[]{:S(2)}) %collective-permute-start.6) | collective-permute-done | bytes 524320 | tf_op jit(solution)/shard_map/ppermute | solution.py:20
  58.9 8.6 collective-permute-done.2
  70.1 8.6 collective-permute-done.8
  84.9 17.2 %collective-permute-done.5 = bf16[512,1024]{1,0:T(8,128)(2,1)S(1)} collective-permute-done((bf16[512,1024]{1,0:T(8,128)(2,1)S(1)}, bf16[512,1024]{1,0:T(8,128)(2,1)S(1)}, u32[]{:S(2)}, u32[]{:S(2)}) %collective-permute-start.5) | collective-permute-done | bytes 1048608 | tf_op jit(solution)/shard_map/ppermute | solution.py:20
  102.1 8.1 fusion.34
  116.1 25.3 %collective-permute-done.3 = bf16[512,1024]{1,0:T(8,128)(2,1)} collective-permute-done((bf16[512,1024]{1,0:T(8,128)(2,1)}, bf16[512,1024]{1,0:T(8,128)(2,1)}, u32[]{:S(2)}, u32[]{:S(2)}) %collective-permute-start.3) | collective-permute-done | bytes 1048608 | tf_op jit(solution)/shard_map/ppermute | solution.py:20
  141.4 6.1 fusion.39
  153.4 6.5 fusion.29
  164.9 9.2 %fusion.84 = (f32[16,512]{1,0:T(8,128)S(1)}, f32[16,512,512]{1,2,0:T(8,128)}) fusion(bf16[512,16,64]{0,2,1:T(8,128)(2,1)} %bitcast.88, bf16[512,16,64]{0,2,1:T(8,128)(2,1)S(1)} %bitcast.86, pred[512]{0:T(512)(128)(4,1)S(1)} %iota_compare_fusion), kind=kOutput, calls=%fused_computation.193 | convolution fusion | flops 549445632 | bytes 18907648 | tf_op jit(solution)/shard_map/qhd,khd->hqk/dot_general | solution.py:48
  174.1 8.4 fusion
  182.5 7.6 fusion.53
  190.1 6.5 fusion.24
  199.9 12.3 %collective-permute-done.10 = bf16[512,1024]{1,0:T(8,128)(2,1)S(1)} collective-permute-done((bf16[512,1024]{1,0:T(8,128)(2,1)S(1)}, bf16[512,1024]{1,0:T(8,128)(2,1)S(1)}, u32[]{:S(2)}, u32[]{:S(2)}) %collective-permute-start.10) | collective-permute-done | bytes 1048608 | tf_op jit(solution)/shard_map/ppermute | solution.py:20
  216.9 45.9 %collective-permute-done.11 = bf16[1024,1024]{1,0:T(8,128)(2,1)} collective-permute-done((bf16[1024,1024]{1,0:T(8,128)(2,1)}, bf16[1024,1024]{1,0:T(8,128)(2,1)}, u32[]{:S(2)}, u32[]{:S(2)}) %collective-permute-start.11) | collective-permute-done | bytes 2097184 | tf_op jit(solution)/shard_map/ppermute | solution.py:20
  262.8 11.8 %fusion.19 = bf16[2048,1024]{1,0:T(8,128)(2,1)S(1)} fusion(s32[]{:T(128)S(6)} %select_n.56, bf16[512,1024]{1,0:T(8,128)(2,1)S(1)} %fusion.52, bf16[512,1024]{1,0:T(8,128)(2,1)} %copy-done.19, bf16[1024,1024]{1,0:T(8,128)(2,1)} %collective-permute-done.11), kind=kLoop, calls=%fused_computation.48 | loop fusion | flops 25165824 | bytes 8388612 | tf_op jit(solution)/shard_map/jit(_roll_dynamic)/concatenate | solution.py:29
  274.6 23.7 %multiply_convert_fusion.1 = (bf16[2048,1024]{1,0:T(8,128)(2,1)S(1)}, f32[2048,1024]{1,0:T(8,128)}, f32[2048,1024]{1,0:T(8,128)}) fusion(f32[1024]{0:T(1024)S(1)} %dynamic-slice_convert_fusion, bf16[2048,1024]{1,0:T(8,128)(2,1)S(1)} %fusion.19, bf16[1024,1024]{1,0:T(8,128)(2,1)S(1)} %copy-done), kind=kOutput, calls=%fused_computation.26 | convolution fusion | flops 4433379328 | bytes 27267072 | tf_op jit(solution)/shard_map/dot_general | solution.py:133
  300.3 6.0 convolution_convert_fusion.1
  307.1 45.9 %reduce-scatter.4.cloned.1.call-done = bf16[512,1024]{1,0:T(8,128)(2,1)} async-done(((bf16[2048,1024]{1,0:T(8,128)(2,1)}), bf16[512,1024]{1,0:T(8,128)(2,1)}) %reduce-scatter.4.cloned.1.call-update) | async-done | bytes 1048592 | tf_op jit(solution)/shard_map/reduce_scatter | solution.py:139
  360.7 12.3 %collective-permute-done.12 = bf16[512,1024]{1,0:T(8,128)(2,1)S(1)} collective-permute-done((bf16[512,1024]{1,0:T(8,128)(2,1)S(1)}, bf16[512,1024]{1,0:T(8,128)(2,1)S(1)}, u32[]{:S(2)}, u32[]{:S(2)}) %collective-permute-start.12) | collective-permute-done | bytes 1048608 | tf_op jit(solution)/shard_map/ppermute | solution.py:20
  374.6 46.6 %collective-permute-done.13 = bf16[1024,1024]{1,0:T(8,128)(2,1)S(1)} collective-permute-done((bf16[1024,1024]{1,0:T(8,128)(2,1)S(1)}, bf16[1024,1024]{1,0:T(8,128)(2,1)S(1)}, u32[]{:S(2)}, u32[]{:S(2)}) %collective-permute-start.13) | collective-permute-done | bytes 2097184 | tf_op jit(solution)/shard_map/ppermute | solution.py:20
  421.2 17.8 %fusion.14 = bf16[2048,1024]{1,0:T(8,128)(2,1)S(1)} fusion(s32[]{:T(128)S(6)} %select_n.56, bf16[512,1024]{1,0:T(8,128)(2,1)S(1)} %get-tuple-element.32, bf16[512,1024]{1,0:T(8,128)(2,1)S(1)} %collective-permute-done.12, bf16[1024,1024]{1,0:T(8,128)(2,1)S(1)} %collective-permute-done.13), kind=kLoop, calls=%fused_computation.43 | loop fusion | flops 25165824 | bytes 8388612 | tf_op jit(solution)/shard_map/jit(_roll_dynamic)/concatenate | solution.py:29
  439.0 13.1 %fusion.72 = (bf16[1024]{0:T(1024)(128)(2,1)S(1)}, bf16[2048,1024]{1,0:T(8,128)(2,1)S(1)}) fusion(f32[2048,1024]{1,0:T(8,128)} %get-tuple-element.42, f32[2048,1024]{1,0:T(8,128)} %get-tuple-element.66, f32[1024]{0:T(1024)S(1)} %dynamic-slice_convert_fusion, bf16[2048,1024]{1,0:T(8,128)(2,1)S(1)} %fusion.14, bf16[1024,1024]{1,0:T(8,128)(2,1)S(1)} %copy-done.54), kind=kOutput, calls=%fused_computation.182 | convolution fusion | flops 4328520704 | bytes 27269120 | tf_op jit(solution)/shard_map/dot_general | solution.py:133
  460.2 46.0 %reduce-scatter.6.cloned.1.call-done = bf16[512,1024]{1,0:T(8,128)(2,1)} async-done(((bf16[2048,1024]{1,0:T(8,128)(2,1)}), bf16[512,1024]{1,0:T(8,128)(2,1)}) %reduce-scatter.6.cloned.1.call-update) | async-done | bytes 1048592 | tf_op jit(solution)/shard_map/reduce_scatter | solution.py:139
  518.3 8.6 bitcast_reduce_fusion
  527.0 11.5 %multiply_reduce_fusion = (f32[16,512]{1,0:T(8,128)S(1)}, f32[16,512,512]{1,2,0:T(8,128)}) fusion(f32[16,512,512]{1,2,0:T(8,128)} %get-tuple-element.63, f32[16,512]{1,0:T(8,128)S(1)} %log_add_fusion, bf16[512,16,64]{0,2,1:T(8,128)(2,1)S(1)} %bitcast.91, bf16[512,16,64]{0,2,1:T(8,128)(2,1)S(1)} %bitcast.93), kind=kOutput, calls=%fused_computation.1 | convolution fusion | flops 549445632 | bytes 35717120 | tf_op jit(solution)/shard_map/qhd,khd->hqk/dot_general | solution.py:74
  538.5 11.8 %multiply_convert_fusion = bf16[16,512,512]{1,2,0:T(8,128)(2,1)S(1)} fusion(f32[16,512,512]{1,2,0:T(8,128)} %get-tuple-element.68, f32[16,512,512]{1,2,0:T(8,128)} %get-tuple-element.63, f32[16,512]{1,0:T(8,128)S(1)} %get-tuple-element.67, f32[16,512]{1,0:T(8,128)S(1)} %log_add_fusion), kind=kLoop, calls=%fused_computation | loop fusion | flops 16777216 | bytes 42008576 | tf_op jit(solution)/shard_map/convert_element_type | solution.py:78
  562.8 8.0 copy.79
  570.8 8.2 convolution_convert_fusion.2
  586.3 56.0 %reduce-scatter.8.cloned.1.call-done = bf16[1024,1024]{1,0:T(8,128)(2,1)} async-done(((bf16[4096,1024]{1,0:T(8,128)(2,1)}), bf16[1024,1024]{1,0:T(8,128)(2,1)}) %reduce-scatter.8.cloned.1.call-update) | async-done | bytes 2097168 | tf_op jit(solution)/shard_map/reduce_scatter | solution.py:139
  651.1 51.5 %all-gather.1 = bf16[32,11,1024]{2,1,0:T(8,128)(2,1)S(1)} all-gather(bf16[1,11,1024]{2,1,0:T(8,128)(2,1)S(1)} %bitcast.106), channel_id=2, replica_groups=mesh['dp'=8,'seq'=4] {'dp','seq'}, dimensions={0}, use_global_device_ids=true | all-gather | bytes 743424 | tf_op jit(solution)/shard_map/all_gather | solution.py:241
  706.6 156.8 %all-reduce.3.cloned.1.call-done = (bf16[1024,1024]{1,0:T(8,128)(2,1)}, bf16[2048,1024]{1,0:T(8,128)(2,1)}) async-done(((bf16[1024,1024]{1,0:T(8,128)(2,1)}, bf16[2048,1024]{1,0:T(8,128)(2,1)}), (bf16[1024,1024]{1,0:T(8,128)(2,1)}, bf16[2048,1024]{1,0:T(8,128)(2,1)})) %all-reduce.3.cloned.1.call-update) | async-done | bytes 6291472 | tf_op jit(solution)/shard_map/psum | solution.py:220
  (226 shorter events, 125.3 us)
Async XLA Ops:
  7.2 267.4 %copy-start = (bf16[1024,1024]{1,0:T(8,128)(2,1)S(1)}, bf16[1024,1024]{1,0:T(8,128)(2,1)}, u32[]{:S(2)}) copy-start(bf16[1024,1024]{1,0:T(8,128)(2,1)} %param.34) | copy-start | bytes 6291460
  7.2 49.0 %copy-start.28 = (bf16[256,1024]{1,0:T(8,128)(2,1)S(1)}, bf16[256,1024]{1,0:T(8,128)(2,1)}, u32[]{:S(2)}) copy-start(bf16[256,1024]{1,0:T(8,128)(2,1)} %param.30) | copy-start | bytes 1572868
  7.2 60.2 %copy-start.27 = (bf16[256,1024]{1,0:T(8,128)(2,1)S(1)}, bf16[256,1024]{1,0:T(8,128)(2,1)}, u32[]{:S(2)}) copy-start(bf16[256,1024]{1,0:T(8,128)(2,1)} %param.31) | copy-start | bytes 1572868
  7.2 345.8 %reduce-scatter.4.cloned.1.call-start = ((), (), s32[]{:S(2)}) async-start(), calls=%async_computation.3 | async-start | bytes 5242880 | tf_op jit(solution)/shard_map/reduce_scatter | solution.py:139
  7.3 9.5 %collective-permute-start = (bf16[256,1024]{1,0:T(8,128)(2,1)}, bf16[256,1024]{1,0:T(8,128)(2,1)S(1)}, u32[]{:S(2)}, u32[]{:S(2)}) collective-permute-start(bf16[256,1024]{1,0:T(8,128)(2,1)} %param.33), channel_id=1, source_target_pairs={{0,3},{1,0},{2,1},{3,2},{4,7},{5,4},{6,5},{7,6},{8,11},{9,8},{10,9... | collective-permute-start | bytes 1572872 | tf_op jit(solution)/shard_map/ppermute | solution.py:20
  9.8 19.0 %collective-permute-start.4 = (bf16[256,1024]{1,0:T(8,128)(2,1)}, bf16[256,1024]{1,0:T(8,128)(2,1)}, u32[]{:S(2)}, u32[]{:S(2)}) collective-permute-start(bf16[256,1024]{1,0:T(8,128)(2,1)} %param.29), channel_id=1, source_target_pairs={{0,3},{1,0},{2,1},{3,2},{4,7},{5,4},{6,5},{7,6},{8,11},{9,8},{10,9... | collective-permute-start | bytes 1572872 | tf_op jit(solution)/shard_map/ppermute | solution.py:20
  19.6 61.7 %collective-permute-start.1 = (bf16[512,1024]{1,0:T(8,128)(2,1)}, bf16[512,1024]{1,0:T(8,128)(2,1)}, u32[]{:S(2)}, u32[]{:S(2)}) collective-permute-start(bf16[512,1024]{1,0:T(8,128)(2,1)} %pad_maximum_fusion.4), channel_id=1, source_target_pairs={{0,2},{1,3},{2,0},{3,1},{4,6},{5,7},{6,4},{7,5},{8,10},{9,11},{10,... | collective-permute-start | bytes 3145736 | tf_op jit(solution)/shard_map/ppermute | solution.py:20
  20.2 36.0 %collective-permute-start.6 = (bf16[256,1024]{1,0:T(8,128)(2,1)}, bf16[256,1024]{1,0:T(8,128)(2,1)}, u32[]{:S(2)}, u32[]{:S(2)}) collective-permute-start(bf16[256,1024]{1,0:T(8,128)(2,1)} %param.30), channel_id=1, source_target_pairs={{0,3},{1,0},{2,1},{3,2},{4,7},{5,4},{6,5},{7,6},{8,11},{9,8},{10,9... | collective-permute-start | bytes 1572872 | tf_op jit(solution)/shard_map/ppermute | solution.py:20
  21.7 45.7 %collective-permute-start.2 = (bf16[256,1024]{1,0:T(8,128)(2,1)}, bf16[256,1024]{1,0:T(8,128)(2,1)}, u32[]{:S(2)}, u32[]{:S(2)}) collective-permute-start(bf16[256,1024]{1,0:T(8,128)(2,1)} %param.31), channel_id=1, source_target_pairs={{0,3},{1,0},{2,1},{3,2},{4,7},{5,4},{6,5},{7,6},{8,11},{9,8},{10,9... | collective-permute-start | bytes 1572872 | tf_op jit(solution)/shard_map/ppermute | solution.py:20
  21.8 56.9 %collective-permute-start.8 = (bf16[256,1024]{1,0:T(8,128)(2,1)}, bf16[256,1024]{1,0:T(8,128)(2,1)}, u32[]{:S(2)}, u32[]{:S(2)}) collective-permute-start(bf16[256,1024]{1,0:T(8,128)(2,1)} %param.32), channel_id=1, source_target_pairs={{0,3},{1,0},{2,1},{3,2},{4,7},{5,4},{6,5},{7,6},{8,11},{9,8},{10,9... | collective-permute-start | bytes 1572872 | tf_op jit(solution)/shard_map/ppermute | solution.py:20
  26.7 52.0 %copy-start.29 = (bf16[256,1024]{1,0:T(8,128)(2,1)S(1)}, bf16[256,1024]{1,0:T(8,128)(2,1)}, u32[]{:S(2)}) copy-start(bf16[256,1024]{1,0:T(8,128)(2,1)} %param.32) | copy-start | bytes 1572868
  28.7 52.7 %copy-start.42 = (bf16[256,1024]{1,0:T(8,128)(2,1)S(1)}, bf16[256,1024]{1,0:T(8,128)(2,1)}, u32[]{:S(2)}) copy-start(bf16[256,1024]{1,0:T(8,128)(2,1)} %param.33) | copy-start | bytes 1572868
  28.7 52.6 %copy-start.44 = (bf16[256,1024]{1,0:T(8,128)(2,1)S(1)}, bf16[256,1024]{1,0:T(8,128)(2,1)}, u32[]{:S(2)}) copy-start(bf16[256,1024]{1,0:T(8,128)(2,1)} %copy-done.43) | copy-start | bytes 1572868
  28.7 52.6 %copy-start.47 = (bf16[1,1024]{1,0:T(2,128)(2,1)S(1)}, bf16[1,1024]{1,0:T(2,128)(2,1)}, u32[]{:S(2)}) copy-start(bf16[1,1024]{1,0:T(2,128)(2,1)} %param.26) | copy-start | bytes 6148
  30.1 72.0 %collective-permute-start.5 = (bf16[512,1024]{1,0:T(8,128)(2,1)S(1)}, bf16[512,1024]{1,0:T(8,128)(2,1)S(1)}, u32[]{:S(2)}, u32[]{:S(2)}) collective-permute-start(bf16[512,1024]{1,0:T(8,128)(2,1)S(1)} %pad_maximum_fusion.6), channel_id=1, source_target_pairs={{0,2},{1,3},{2,0},{3,1},{4,6},{5,7},{6,4},{7,5},{8,10},{9,11},{10,... | collective-permute-start | bytes 3145736 | tf_op jit(solution)/shard_map/ppermute | solution.py:20
  58.3 95.1 %collective-permute-start.7 = (bf16[512,1024]{1,0:T(8,128)(2,1)}, bf16[512,1024]{1,0:T(8,128)(2,1)}, u32[]{:S(2)}, u32[]{:S(2)}) collective-permute-start(bf16[512,1024]{1,0:T(8,128)(2,1)} %pad_maximum_fusion.7), channel_id=1, source_target_pairs={{0,2},{1,3},{2,0},{3,1},{4,6},{5,7},{6,4},{7,5},{8,10},{9,11},{10,... | collective-permute-start | bytes 3145736 | tf_op jit(solution)/shard_map/ppermute | solution.py:20
  69.5 71.9 %collective-permute-start.3 = (bf16[512,1024]{1,0:T(8,128)(2,1)}, bf16[512,1024]{1,0:T(8,128)(2,1)}, u32[]{:S(2)}, u32[]{:S(2)}) collective-permute-start(bf16[512,1024]{1,0:T(8,128)(2,1)} %pad_maximum_fusion.5), channel_id=1, source_target_pairs={{0,2},{1,3},{2,0},{3,1},{4,6},{5,7},{6,4},{7,5},{8,10},{9,11},{10,... | collective-permute-start | bytes 3145736 | tf_op jit(solution)/shard_map/ppermute | solution.py:20
  80.8 109.3 %collective-permute-start.9 = (bf16[512,1024]{1,0:T(8,128)(2,1)}, bf16[512,1024]{1,0:T(8,128)(2,1)}, u32[]{:S(2)}, u32[]{:S(2)}) collective-permute-start(bf16[512,1024]{1,0:T(8,128)(2,1)} %pad_maximum_fusion.8), channel_id=1, source_target_pairs={{0,2},{1,3},{2,0},{3,1},{4,6},{5,7},{6,4},{7,5},{8,10},{9,11},{10,... | collective-permute-start | bytes 3145736 | tf_op jit(solution)/shard_map/ppermute | solution.py:20
  84.8 26.7 %copy-start.33 = (bf16[512,1024]{1,0:T(8,128)(2,1)S(1)}, bf16[512,1024]{1,0:T(8,128)(2,1)}, u32[]{:S(2)}) copy-start(bf16[512,1024]{1,0:T(8,128)(2,1)} %param.25) | copy-start | bytes 3145732
  84.9 111.8 %copy-start.45 = (f32[1024]{0:T(1024)}, f32[1024]{0:T(1024)S(1)}, u32[]{:S(2)}) copy-start(f32[1024]{0:T(1024)S(1)} %convert_add_fusion.2) | copy-start | bytes 12292
  116.1 32.8 %copy-start.34 = (bf16[512,1024]{1,0:T(8,128)(2,1)S(1)}, bf16[512,1024]{1,0:T(8,128)(2,1)}, u32[]{:S(2)}) copy-start(bf16[512,1024]{1,0:T(8,128)(2,1)} %param.25) | copy-start | bytes 3145732
  199.8 12.4 %collective-permute-start.10 = (bf16[512,1024]{1,0:T(8,128)(2,1)S(1)}, bf16[512,1024]{1,0:T(8,128)(2,1)S(1)}, u32[]{:S(2)}, u32[]{:S(2)}) collective-permute-start(bf16[512,1024]{1,0:T(8,128)(2,1)S(1)} %fusion.52), channel_id=1, source_target_pairs={{0,3},{1,0},{2,1},{3,2},{4,7},{5,4},{6,5},{7,6},{8,11},{9,8},{10,9... | collective-permute-start | bytes 3145736 | tf_op jit(solution)/shard_map/ppermute | solution.py:20
  214.8 48.0 %collective-permute-start.11 = (bf16[1024,1024]{1,0:T(8,128)(2,1)}, bf16[1024,1024]{1,0:T(8,128)(2,1)}, u32[]{:S(2)}, u32[]{:S(2)}) collective-permute-start(bf16[1024,1024]{1,0:T(8,128)(2,1)} %pad_maximum_fusion.2), channel_id=1, source_target_pairs={{0,2},{1,3},{2,0},{3,1},{4,6},{5,7},{6,4},{7,5},{8,10},{9,11},{10,... | collective-permute-start | bytes 6291464 | tf_op jit(solution)/shard_map/ppermute | solution.py:20
  274.6 25.7 %copy-start.53 = (bf16[1024,1024]{1,0:T(8,128)(2,1)S(1)}, bf16[1024,1024]{1,0:T(8,128)(2,1)}, u32[]{:S(2)}) copy-start(bf16[1024,1024]{1,0:T(8,128)(2,1)} %param.35) | copy-start | bytes 6291460
  306.4 49.6 %copy-start.18 = (bf16[512,1024]{1,0:T(8,128)(2,1)S(1)}, bf16[512,1024]{1,0:T(8,128)(2,1)}, u32[]{:S(2)}) copy-start(bf16[512,1024]{1,0:T(8,128)(2,1)} %param.28) | copy-start | bytes 3145732
  306.4 199.8 %reduce-scatter.6.cloned.1.call-start = ((), (), s32[]{:S(2)}) async-start(), calls=%async_computation.4 | async-start | bytes 5242880 | tf_op jit(solution)/shard_map/reduce_scatter | solution.py:139
  360.6 12.4 %collective-permute-start.12 = (bf16[512,1024]{1,0:T(8,128)(2,1)S(1)}, bf16[512,1024]{1,0:T(8,128)(2,1)S(1)}, u32[]{:S(2)}, u32[]{:S(2)}) collective-permute-start(bf16[512,1024]{1,0:T(8,128)(2,1)S(1)} %get-tuple-element.32), channel_id=1, source_target_pairs={{0,3},{1,0},{2,1},{3,2},{4,7},{5,4},{6,5},{7,6},{8,11},{9,8},{10,9... | collective-permute-start | bytes 3145736 | tf_op jit(solution)/shard_map/ppermute | solution.py:20
  373.2 65.8 %copy-start.54 = (bf16[1024,1024]{1,0:T(8,128)(2,1)S(1)}, bf16[1024,1024]{1,0:T(8,128)(2,1)}, u32[]{:S(2)}) copy-start(bf16[1024,1024]{1,0:T(8,128)(2,1)} %param.35) | copy-start | bytes 6291460
  373.2 48.0 %collective-permute-start.13 = (bf16[1024,1024]{1,0:T(8,128)(2,1)S(1)}, bf16[1024,1024]{1,0:T(8,128)(2,1)S(1)}, u32[]{:S(2)}, u32[]{:S(2)}) collective-permute-start(bf16[1024,1024]{1,0:T(8,128)(2,1)S(1)} %pad_maximum_fusion.3), channel_id=1, source_target_pairs={{0,2},{1,3},{2,0},{3,1},{4,6},{5,7},{6,4},{7,5},{8,10},{9,11},{10,... | collective-permute-start | bytes 6291464 | tf_op jit(solution)/shard_map/ppermute | solution.py:20
  460.1 182.2 %reduce-scatter.8.cloned.1.call-start = ((), (), s32[]{:S(2)}) async-start(), calls=%async_computation.5 | async-start | bytes 10485760 | tf_op jit(solution)/shard_map/reduce_scatter | solution.py:139
  527.0 27.5 %copy-start.40 = (bf16[16,64,512]{2,1,0:T(8,128)(2,1)}, bf16[16,64,512]{2,1,0:T(8,128)(2,1)S(1)}, u32[]{:S(2)}) copy-start(bf16[16,64,512]{2,1,0:T(8,128)(2,1)S(1)} %get-tuple-element.73) | copy-start | bytes 3145732
  570.8 292.6 %all-reduce.3.cloned.1.call-start = ((), (), s32[]{:S(2)}) async-start(), calls=%async_computation.6 | async-start | bytes 12582912 | tf_op jit(solution)/shard_map/psum | solution.py:220
  (44 other events, 209.1 us)
Sparse Core Ops, SparseCore 0:
  306.5 46.4 reduce-scatter.3
  460.2 45.8 reduce-scatter.5
  570.9 71.3 reduce-scatter.7
  646.7 216.6 all-reduce.2
